TPU v7x, 32 devices: a whole 2x2x4 slice. The times are simulated.
32 devices in a mesh: dp: 4 (over y, core), blk: 4 (over z), ulysses: 2 (over x).
Axes of the slice: x: 2, y: 2, z: 4, core: 2. Of those that a mesh axis runs over, the one named last changes fastest.
Arguments:
- queries: bfloat16 [24576, 2048], P(('dp', 'blk', 'ulysses')), parts along dimension 0, may hold values from -128 to 128
- keys: bfloat16 [24576, 2048], P(('dp', 'blk', 'ulysses')), parts along dimension 0, may hold values from -6 to 6
- values: bfloat16 [24576, 2048], P(('dp', 'blk', 'ulysses')), parts along dimension 0, may hold values from -6 to 6
- rel_bias: float32 [16, 27], replicated, may hold values from -4 to 4
- tile_lists: int32 [16, 8], replicated, may hold values from 0 to 16, as said below
- tile_pos: int32 [16], replicated, may hold values from 0 to 3, as said below
Outputs:
- attended: bfloat16 [24576, 2048], P(('dp', 'blk', 'ulysses')), parts along dimension 0
There are 4 independent parts, one for each index of `dp`. A program takes and returns all parts, laid end to end along the dimension named above; an argument that names none is the same for every part. Nothing has to cross between parts.
Inputs may be any that keep to these rules, and one draw needn't show every extreme that they name: `tile_lists`: row t names the key tiles of query tile t, each once: t itself first, then tiles of t's frame or of the frames just before and after it (frame = tile // 4); named tiles come first and 16 fills the rest of the row. `tile_pos`: the cell (row * 2 + column) of each tile within its frame; the tiles of one frame take each cell once.
All inputs are finite; a program needn't handle non-finite values.
Results may differ from a plain program's by a relative error of at most 0.0035.
Values may be sent and summed in bfloat16 or wider, within the bound.
A program may use at most 128 MiB of HBM per device.

v0:
```python
import math

import jax
import jax.numpy as jnp
from jax import lax
from jax.sharding import PartitionSpec as P

H = 16
DH = 128
TILE = 384
GH = 2
GW = 2
FB = 1


def with_halo(cells, sides, width):
    for axis, dim in sides:
        count = lax.axis_size(axis)
        ends = count - 1
        head = lax.slice_in_dim(cells, 0, width, axis=dim)
        tail = lax.slice_in_dim(cells, cells.shape[dim] - width, cells.shape[dim], axis=dim)
        cells = jnp.concatenate(
            [
                lax.ppermute(tail, axis, [(i, (i + 1) % count) for i in range(ends)]),
                cells,
                lax.ppermute(head, axis, [((i + 1) % count, i) for i in range(ends)]),
            ],
            axis=dim,
        )
    return cells


def on_device(queries, keys, values, rel_bias, tile_lists, tile_pos):
    uly_count = lax.axis_size("ulysses")
    blk_rank = lax.axis_index("blk")
    uly_rank = lax.axis_index("ulysses")
    heads_dev = H // uly_count
    head_cols = heads_dev * DH
    frame_tiles = GH * GW
    local_tiles = FB * frame_tiles
    total_tiles = tile_lists.shape[0]
    inv_root = 1.0 / math.sqrt(DH)
    q_heads, k_heads, v_heads = (
        lax.all_to_all(queries, "ulysses", split_axis=1, concat_axis=0, tiled=True),
        lax.all_to_all(keys, "ulysses", split_axis=1, concat_axis=0, tiled=True),
        lax.all_to_all(values, "ulysses", split_axis=1, concat_axis=0, tiled=True),
    )
    paired = jnp.stack((k_heads, v_heads))
    widened = with_halo(paired, (("blk", 1),), frame_tiles * TILE)
    lead_frames = 1
    buffer_tiles = widened.shape[1] // TILE
    first_tile = (blk_rank * FB - lead_frames) * frame_tiles
    my_lists = lax.dynamic_slice_in_dim(tile_lists, blk_rank * local_tiles, local_tiles, 0)
    head_table = lax.dynamic_slice_in_dim(rel_bias, uly_rank * heads_dev, heads_dev, 0)
    q_tiles = q_heads.reshape(local_tiles, TILE, heads_dev, DH)
    query_ids = [blk_rank * local_tiles + within for within in range(local_tiles)]
    query_cells = [tile_pos[qid] for qid in query_ids]

    def bias_for(tile_slot, key_id):
        safe_id = jnp.clip(key_id, 0, total_tiles - 1)
        key_cell = tile_pos[safe_id]
        query_cell = query_cells[tile_slot]
        offset = (safe_id // frame_tiles - query_ids[tile_slot] // frame_tiles + 1) * 9
        offset = offset + (key_cell // GW - query_cell // GW + 1) * 3
        offset = offset + (key_cell % GW - query_cell % GW + 1)
        offset = jnp.clip(offset, 0, 26)
        return lax.dynamic_index_in_dim(head_table, offset, 1, keepdims=False)

    def attend(tile_state, tile_slot, key_id, allowed, key_block, value_block):
        old_max, old_total, accum_out = tile_state
        scores = (
            jnp.einsum(
                "ihd,jhd->hij", q_tiles[tile_slot], key_block, preferred_element_type=jnp.float32
            )
            * inv_root
        )
        scores = scores + bias_for(tile_slot, key_id)[:, None, None]
        scores = jnp.where(allowed, scores, -1e30)
        new_max = jnp.maximum(old_max, jnp.max(scores, axis=2))
        weights = jnp.where(allowed, jnp.exp(scores - new_max[..., None]), 0.0)
        rescale = jnp.exp(old_max - new_max)
        new_total = old_total * rescale + jnp.sum(weights, axis=2)
        product = jnp.einsum(
            "hij,jhd->ihd",
            weights.astype(jnp.bfloat16),
            value_block,
            preferred_element_type=jnp.float32,
        )
        accum_out = accum_out * jnp.transpose(rescale)[:, :, None] + product
        return (new_max, new_total, accum_out)

    def fetch(local_id):
        block = lax.dynamic_slice(widened, (0, local_id * TILE, 0), (2, TILE, head_cols))
        return (block[0].reshape(TILE, heads_dev, DH), block[1].reshape(TILE, heads_dev, DH))

    def by_slot(slot_index, states):
        key_ids = lax.dynamic_index_in_dim(my_lists, slot_index, 1, keepdims=False)
        updated = []
        for tile_slot in range(local_tiles):
            key_id = key_ids[tile_slot]
            valid = key_id < total_tiles
            local_id = jnp.clip(key_id - first_tile, 0, buffer_tiles - 1)
            key_block, value_block = fetch(local_id)
            updated.append(
                attend(states[tile_slot], tile_slot, key_id, valid, key_block, value_block)
            )
        return tuple(updated)

    initial = tuple(
        (
            (
                jnp.full((heads_dev, TILE), -1e30, jnp.float32),
                jnp.zeros((heads_dev, TILE), jnp.float32),
                jnp.zeros((TILE, heads_dev, DH), jnp.float32),
            )
            for tile_slot in range(local_tiles)
        )
    )
    live_slots = jnp.max(jnp.sum((my_lists < total_tiles).astype(jnp.int32), axis=1))
    final_state = lax.fori_loop(0, live_slots, by_slot, initial)
    pieces = []
    for tile_slot in range(local_tiles):
        tile_total = jnp.transpose(final_state[tile_slot][1])
        mixed_tile = (final_state[tile_slot][2] / tile_total[:, :, None]).astype(jnp.bfloat16)
        pieces.append(mixed_tile.reshape(TILE, head_cols))
    mixed = jnp.concatenate(pieces, axis=0)
    return lax.all_to_all(mixed, "ulysses", split_axis=0, concat_axis=1, tiled=True)


def solution(mesh):
    return jax.shard_map(
        on_device,
        mesh=mesh,
        in_specs=(
            P(("dp", "blk", "ulysses"), None),
            P(("dp", "blk", "ulysses"), None),
            P(("dp", "blk", "ulysses"), None),
            P(),
            P(),
            P(),
        ),
        out_specs=P(("dp", "blk", "ulysses"), None),
        check_vma=False,
    )
```

profile of v0, /device:TPU:8, one launch (start us, length us, event | category | flops | bytes accessed | tf_op | source)
XLA Modules:
  0.0 775.0 jit_solution(13200815248339285674)
XLA Ops:
  0.0 4.7 copy.102
  4.7 3.9 all-to-all-start
  8.6 4.6 copy.104
  13.3 31.7 %all-to-all-done = bf16[768,2,1024]{0,2,1:T(8,128)(2,1)S(1)} async-done(((bf16[768,2,1024]{0,2,1:T(8,128)(2,1)}), bf16[768,2,1024]{0,2,1:T(8,128)(2,1)S(1)}, u32[]{:S(2)}, u32[]{:S(2)}) %all-to-all-start) | async-done | bytes 3145760 | tf_op jit(solution)/shard_map/all_to_all | solution.py:45
  46.6 5.2 all-to-all-start.1
  51.8 3.2 copy.103
  55.0 32.4 %all-to-all-done.1 = bf16[768,2,1024]{0,2,1:T(8,128)(2,1)} async-done(((bf16[768,2,1024]{0,2,1:T(8,128)(2,1)}), bf16[768,2,1024]{0,2,1:T(8,128)(2,1)}, u32[]{:S(2)}, u32[]{:S(2)}) %all-to-all-start.1) | async-done | bytes 3145760 | tf_op jit(solution)/shard_map/all_to_all | solution.py:46
  87.4 4.6 copy.105
  92.1 5.2 pad_maximum_fusion.1
  97.3 3.5 collective-permute-start
  100.7 4.9 collective-permute-start.1
  107.7 5.3 all-to-all-start.2
  125.1 22.1 %all-to-all-done.2 = bf16[768,2,1024]{2,0,1:T(8,128)(2,1)} async-done(((bf16[768,2,1024]{2,0,1:T(8,128)(2,1)}), bf16[768,2,1024]{2,0,1:T(8,128)(2,1)}, u32[]{:S(2)}, u32[]{:S(2)}) %all-to-all-start.2) | async-done | bytes 3145760 | tf_op jit(solution)/shard_map/all_to_all | solution.py:44
  147.2 2.7 copy.131
  152.3 82.7 %collective-permute-done = bf16[2,1536,1024]{2,1,0:T(8,128)(2,1)} collective-permute-done((bf16[2,1536,1024]{2,1,0:T(8,128)(2,1)}, bf16[2,1536,1024]{2,1,0:T(8,128)(2,1)}, u32[]{:S(2)}, u32[]{:S(2)}) %collective-permute-start) | collective-permute-done | bytes 6291488 | tf_op jit(solution)/shard_map/ppermute | solution.py:24
  235.0 3.8 collective-permute-done.1
  238.8 13.5 %pad_maximum_fusion = bf16[2,4608,1024]{2,1,0:T(8,128)(2,1)} fusion(bf16[2,1536,1024]{2,1,0:T(8,128)(2,1)} %collective-permute-done.1, bf16[1,1536,1024]{2,1,0:T(8,128)(2,1)S(1)} %bitcast.261, bf16[1,1536,1024]{2,1,0:T(8,128)(2,1)S(1)} %bitcast.259, bf16[2,1536,1024]{2,1,0:T(8,128)(2,1)} %collective-permute-done), kind=kLoop, calls=%fused_computation.97 | loop fusion | flops 75497472 | bytes 37748736 | tf_op jit(solution)/shard_map/concatenate | solution.py:22
  252.2 24.8 %copy.108 = bf16[2,4608,1024]{1,2,0:T(8,128)(2,1)} copy(bf16[2,4608,1024]{2,1,0:T(8,128)(2,1)} %pad_maximum_fusion) | data formatting | bytes 37748736 | tf_op jit(solution)/shard_map/while | solution.py:120
  282.3 437.9 %while.36 = (s32[]{:T(128)}, f32[8,384]{1,0:T(8,128)S(1)}, f32[8,384]{1,0:T(8,128)S(1)}, f32[384,8,128]{0,2,1:T(8,128)}, f32[8,384]{1,0:T(8,128)S(1)}, /*index=5...) while((s32[]{:T(128)}, f32[8,384]{1,0:T(8,128)S(1)}, ...), condition=%wide.region_11.12_spmd, body=%wide.region_2.11_spmd.sunk | while | flops 2494599424 | bytes 202116768 | solution.py:120
  300.2 5.0 constant_dynamic-slice_fusion.18
  305.9 2.8 bitcast_reduce_fusion.11
  312.7 2.9 bitcast_reduce_fusion.10
  315.6 4.2 bitcast_add_fusion.10
  329.8 2.6 bitcast_reduce_fusion.8
  354.8 5.0 constant_dynamic-slice_fusion.18
  360.5 2.8 bitcast_reduce_fusion.11
  367.3 2.9 bitcast_reduce_fusion.10
  370.2 4.2 bitcast_add_fusion.10
  384.4 2.6 bitcast_reduce_fusion.8
  409.4 5.0 constant_dynamic-slice_fusion.18
  415.1 2.8 bitcast_reduce_fusion.11
  421.9 2.9 bitcast_reduce_fusion.10
  424.8 4.2 bitcast_add_fusion.10
  439.0 2.6 bitcast_reduce_fusion.8
  464.0 5.1 constant_dynamic-slice_fusion.18
  469.8 2.8 bitcast_reduce_fusion.11
  476.6 2.9 bitcast_reduce_fusion.10
  479.5 4.2 bitcast_add_fusion.10
  493.7 2.6 bitcast_reduce_fusion.8
  518.7 5.0 constant_dynamic-slice_fusion.18
  524.4 2.8 bitcast_reduce_fusion.11
  531.2 2.9 bitcast_reduce_fusion.10
  534.1 4.2 bitcast_add_fusion.10
  548.3 2.6 bitcast_reduce_fusion.8
  573.3 5.0 constant_dynamic-slice_fusion.18
  579.0 2.8 bitcast_reduce_fusion.11
  585.8 2.9 bitcast_reduce_fusion.10
  588.7 4.2 bitcast_add_fusion.10
  602.9 2.6 bitcast_reduce_fusion.8
  627.9 5.0 constant_dynamic-slice_fusion.18
  633.6 2.8 bitcast_reduce_fusion.11
  640.4 2.9 bitcast_reduce_fusion.10
  643.3 4.2 bitcast_add_fusion.10
  657.5 2.6 bitcast_reduce_fusion.8
  682.5 5.0 constant_dynamic-slice_fusion.18
  688.2 2.8 bitcast_reduce_fusion.11
  695.0 2.9 bitcast_reduce_fusion.10
  697.9 4.2 bitcast_add_fusion.10
  712.1 2.6 bitcast_reduce_fusion.8
  720.2 3.2 divide_convert_fusion.2
  725.2 3.0 divide_convert_fusion
  731.4 36.1 %all_to_all.67 = bf16[2,768,1024]{2,1,0:T(8,128)(2,1)S(1)} all-to-all(bf16[2,768,1024]{2,1,0:T(8,128)(2,1)S(1)} %bitcast.273), channel_id=1, replica_groups=mesh['dp'=4,'blk'=4,'ulysses'=2] {'ulysses'}, dimensions={0} | all-to-all | bytes 6291456 | tf_op jit(solution)/shard_map/all_to_all | solution.py:127
  767.5 2.8 copy.114
  770.3 4.6 copy.115
  (458 shorter events, 160.4 us)
Async XLA Ops:
  0.0 124.2 %copy-start = (f32[16,27]{1,0:T(8,128)S(1)}, f32[16,27]{1,0:T(8,128)}, u32[]{:S(2)}) copy-start(f32[16,27]{1,0:T(8,128)} %param.11) | copy-start | bytes 5188
  4.7 40.3 %all-to-all-start = ((bf16[768,2,1024]{0,2,1:T(8,128)(2,1)}), bf16[768,2,1024]{0,2,1:T(8,128)(2,1)S(1)}, u32[]{:S(2)}, u32[]{:S(2)}) async-start(bf16[768,2,1024]{0,2,1:T(8,128)(2,1)} %bitcast.272), calls=%async_computation | async-start | bytes 6291456 | tf_op jit(solution)/shard_map/all_to_all | solution.py:45
  46.6 40.8 %all-to-all-start.1 = ((bf16[768,2,1024]{0,2,1:T(8,128)(2,1)}), bf16[768,2,1024]{0,2,1:T(8,128)(2,1)}, u32[]{:S(2)}, u32[]{:S(2)}) async-start(bf16[768,2,1024]{0,2,1:T(8,128)(2,1)} %bitcast.271), calls=%async_computation.1 | async-start | bytes 6291456 | tf_op jit(solution)/shard_map/all_to_all | solution.py:46
  92.1 13.6 %copy-start.15 = (bf16[768,2048]{1,0:T(8,128)(2,1)S(1)}, bf16[768,2048]{1,0:T(8,128)(2,1)}, u32[]{:S(2)}) copy-start(bf16[768,2048]{1,0:T(8,128)(2,1)} %param.8) | copy-start | bytes 9437188
  97.3 137.7 %collective-permute-start = (bf16[2,1536,1024]{2,1,0:T(8,128)(2,1)}, bf16[2,1536,1024]{2,1,0:T(8,128)(2,1)}, u32[]{:S(2)}, u32[]{:S(2)}) collective-permute-start(bf16[2,1536,1024]{2,1,0:T(8,128)(2,1)} %pad_maximum_fusion.1), channel_id=1, source_target_pairs={{0,2},{2,4},{4,6},{1,3},{3,5},{5,7},{8,10},{10,12},{12,14},{9,11},... | collective-permute-start | bytes 18874376 | tf_op jit(solution)/shard_map/ppermute | solution.py:24
  100.7 138.0 %collective-permute-start.1 = (bf16[2,1536,1024]{2,1,0:T(8,128)(2,1)}, bf16[2,1536,1024]{2,1,0:T(8,128)(2,1)}, u32[]{:S(2)}, u32[]{:S(2)}) collective-permute-start(bf16[2,1536,1024]{2,1,0:T(8,128)(2,1)} %pad_maximum_fusion.1), channel_id=1, source_target_pairs={{2,0},{4,2},{6,4},{3,1},{5,3},{7,5},{10,8},{12,10},{14,12},{11,9},... | collective-permute-start | bytes 18874376 | tf_op jit(solution)/shard_map/ppermute | solution.py:26
  107.7 5.4 copy-start.16
  107.7 16.3 %copy-start.17 = (s32[16,8]{0,1:T(8,128)S(1)}, s32[16,8]{0,1:T(8,128)}, u32[]{:S(2)}) copy-start(s32[16,8]{0,1:T(8,128)} %param.12) | copy-start | bytes 1540
  107.7 39.5 %all-to-all-start.2 = ((bf16[768,2,1024]{2,0,1:T(8,128)(2,1)}), bf16[768,2,1024]{2,0,1:T(8,128)(2,1)}, u32[]{:S(2)}, u32[]{:S(2)}) async-start(bf16[768,2,1024]{2,0,1:T(8,128)(2,1)} %bitcast.270), calls=%async_computation.2 | async-start | bytes 6291456 | tf_op jit(solution)/shard_map/all_to_all | solution.py:44
  149.9 88.9 %copy-start.4 = (bf16[768,2,1024]{2,0,1:T(8,128)(2,1)S(1)}, bf16[768,2,1024]{2,0,1:T(8,128)(2,1)}, u32[]{:S(2)}) copy-start(bf16[768,2,1024]{2,0,1:T(8,128)(2,1)} %copy.105) | copy-start | bytes 9437188
  312.7 2.9 copy-start.5
  312.7 7.1 slice-start.2
  315.6 4.2 slice-start.3
  328.0 4.5 copy-start.8
  329.8 5.8 slice-start
  332.5 3.1 slice-start.1
  360.5 2.9 copy-start.6
  360.5 2.9 copy-start.12
  367.3 2.9 copy-start.5
  367.3 7.1 slice-start.2
  370.2 4.2 slice-start.3
  382.6 4.5 copy-start.8
  384.4 5.8 slice-start
  387.1 3.1 slice-start.1
  421.9 2.9 copy-start.5
  421.9 7.1 slice-start.2
  424.8 4.2 slice-start.3
  437.2 4.5 copy-start.8
  439.0 5.8 slice-start
  441.7 3.1 slice-start.1
  476.6 2.9 copy-start.5
  476.6 7.1 slice-start.2
  479.5 4.2 slice-start.3
  491.9 4.5 copy-start.8
  493.7 5.8 slice-start
  496.4 3.1 slice-start.1
  531.2 2.9 copy-start.5
  531.2 7.1 slice-start.2
  534.1 4.2 slice-start.3
  546.5 4.5 copy-start.8
  548.3 5.8 slice-start
  551.0 3.1 slice-start.1
  585.8 2.9 copy-start.5
  585.8 7.1 slice-start.2
  588.7 4.2 slice-start.3
  601.1 4.5 copy-start.8
  602.9 5.8 slice-start
  605.6 3.1 slice-start.1
  633.6 2.9 copy-start.6
  633.6 2.9 copy-start.12
  640.4 2.9 copy-start.5
  640.4 7.1 slice-start.2
  643.3 4.2 slice-start.3
  655.7 4.5 copy-start.8
  657.5 5.8 slice-start
  660.2 3.1 slice-start.1
  695.0 2.9 copy-start.5
  695.0 7.1 slice-start.2
  697.9 4.2 slice-start.3
  710.3 4.5 copy-start.8
  712.1 5.8 slice-start
  714.8 3.1 slice-start.1
  720.2 5.0 copy-start.14
  767.5 7.4 copy-start.1
  (61 other events, 133.1 us)
where the time goes:
time: 780 us; the launch traced here: 775 us
  waiting for transfers between devices  173 us (22%)
  matrix products  162 us (21%)
  loops' own time  155 us (20%)
  local copies, waits for them, and re-layouts  146 us (19%)
  other arithmetic  69.4 us (9%)
  blocking collectives  36.1 us (5%)
  starting transfers between devices  22.9 us (3%)
  between operations  10.5 us (1%)
    another operation x1, loops' own time, on_device(): final_state = lax.fori_loop(0, live_slots, by_slot, initial)  155 us
    dot_general x32, matrix products, attend(): jnp.einsum('ihd,jhd->hij', q_tiles[tile_slot], key_block, preferred_eleme...  87.1 us
    ppermute x1, waiting for transfers between devices, with_halo(): lax.ppermute(tail, axis, [(i, (i + 1) % count) for i in range(ends)])  82.7 us
    dot_general x32, matrix products, attend(): jnp.einsum('hij,jhd->ihd', weights.astype(jnp.bfloat16), value_block, pre...  75 us
    reduce_sum x32, other arithmetic, attend(): new_total = old_total * rescale + jnp.sum(weights, axis=2)  42.7 us
    slice x8, local copies, waits for them, and re-layouts, fetch(): block[1].reshape(TILE, heads_dev, DH)  40.1 us
    all_to_all x1, blocking collectives, on_device(): lax.all_to_all(mixed, 'ulysses', split_axis=0, concat_axis=1, tiled=True)  36.1 us
    all_to_all x1, waiting for transfers between devices, on_device(): lax.all_to_all(values, 'ulysses', split_axis=1, concat_axis=0, tiled=True)  32.4 us
  transfers between devices with their start and end apart: 5, of which 5 were waited for; matrix products, arithmetic and copies ran while one was open for 2% of the time, Pallas kernels for 0%

commit v1 on v0

v1 whole, which is shorter than its diff:
```python
import functools
import math

import jax
import jax.numpy as jnp
from jax import lax
from jax.experimental import pallas as pl
from jax.experimental.pallas import tpu as pltpu
from jax.sharding import PartitionSpec as P

H = 16
DH = 128
TILE = 384
GH = 2
GW = 2
LOG2E = 1.4426950408889634
MESH = pl.DeviceIdType.MESH


def attention_kernel(n, blk_count, groups, tokens, slots, *refs):
    lists_ref, bias_ref, q_ref, k_ref, v_ref, out_ref = refs[:6]
    k_bufs = refs[6 : 6 + groups]
    v_bufs = refs[6 + groups : 6 + 2 * groups]
    q_bufs = refs[6 + 2 * groups : 6 + 3 * groups]
    o_bufs = refs[6 + 3 * groups : 6 + 4 * groups]
    s_buf, acc, local_sems, x_send, x_recv, z_send, z_recv, o_send, o_recv = refs[6 + 4 * groups :]
    frame = tokens * n
    head_cols = groups * DH
    rank = lax.axis_index("ulysses")
    blk = lax.axis_index("blk")
    has_up = blk < blk_count - 1
    has_down = blk > 0
    scale = LOG2E / math.sqrt(DH)
    inputs = (k_ref, v_ref, q_ref)

    unit = math.gcd(tokens, TILE)
    parts = TILE // unit

    def rows(frame_index, owner):
        return pl.ds(frame_index * (frame // unit) + owner * (tokens // unit), tokens // unit)

    def flat(owner):
        return pl.ds(pl.multiple_of(owner * tokens, 64), tokens)

    def lanes(owner, g):
        return pl.ds(pl.multiple_of(owner * head_cols + g * DH, DH), DH)

    def cut(which, owner, g):
        if which == 2:
            return q_ref.at[:, lanes(owner, g)]
        return inputs[which].at[:, :, lanes(owner, g)]

    def home(which, g, owner):
        if which == 2:
            return q_bufs[g].at[flat(owner)]
        return (k_bufs, v_bufs)[which][g].at[rows(1, owner)]

    def local(which, g):
        return pltpu.make_async_copy(
            cut(which, rank, g), home(which, g, rank), local_sems.at[which, g]
        )

    def across(which, g, d):
        target = lax.rem(rank + d, n)
        return pltpu.make_async_remote_copy(
            src_ref=cut(which, target, g),
            dst_ref=home(which, g, rank),
            send_sem=x_send.at[which, g, d],
            recv_sem=x_recv.at[which, g, d],
            device_id={"ulysses": target},
            device_id_type=MESH,
        )

    def halo(which, g, d, way):
        owner = lax.rem(rank + (n - d), n)
        source = home(which, g, owner) if d else cut(which, rank, g)
        return pltpu.make_async_remote_copy(
            src_ref=source,
            dst_ref=(k_bufs, v_bufs)[which][g].at[rows(2 * way, owner)],
            send_sem=z_send.at[way, which, g, d],
            recv_sem=z_recv.at[way, which, g, d],
            device_id={"blk": blk - 1 if way else blk + 1},
            device_id_type=MESH,
        )

    def give(g, d):
        target = lax.rem(rank + d, n)
        return pltpu.make_async_remote_copy(
            src_ref=o_bufs[g].at[flat(target)],
            dst_ref=out_ref.at[:, lanes(rank, g)],
            send_sem=o_send.at[g, d],
            recv_sem=o_recv.at[g, d],
            device_id={"ulysses": target},
            device_id_type=MESH,
        )

    def keep(g):
        return pltpu.make_async_copy(
            o_bufs[g].at[flat(rank)], out_ref.at[:, lanes(rank, g)], o_send.at[g, 0]
        )

    def start_halo(g, ds):
        for way, present in ((0, has_up), (1, has_down)):
            @pl.when(present)
            def _():
                for d in ds:
                    for which in range(2):
                        halo(which, g, d, way).start()

    def relay(g):
        for d in range(1, n):
            for which in range(2):
                across(which, g, d).wait_recv()
        start_halo(g, range(1, n))

    barrier = pltpu.get_barrier_semaphore()
    for d in range(1, n):
        pl.semaphore_signal(
            barrier, inc=1, device_id={"ulysses": lax.rem(rank + d, n)}, device_id_type=MESH
        )
    @pl.when(has_up)
    def _():
        pl.semaphore_signal(barrier, inc=1, device_id={"blk": blk + 1}, device_id_type=MESH)
    @pl.when(has_down)
    def _():
        pl.semaphore_signal(barrier, inc=1, device_id={"blk": blk - 1}, device_id_type=MESH)
    below = (blk + blk_count - 1) // blk_count
    above = (2 * blk_count - 2 - blk) // blk_count
    pl.semaphore_wait(barrier, n - 1 + below + above)

    for g in range(groups):
        for which in range(3):
            for d in range(1, n):
                across(which, g, d).start()
        if g == 0:
            start_halo(0, range(1))
    for g in range(groups):
        for which in range(3):
            local(which, g).start()
    relay(0)
    if groups > 1:
        start_halo(1, range(1))

    pairs = slots // 2
    ones = jnp.ones((2 * TILE, DH), jnp.bfloat16)

    def compute(g):
        k_buf, v_buf, q_buf, o_buf = k_bufs[g], v_bufs[g], q_bufs[g], o_bufs[g]

        def listed(buf, t, p):
            return jnp.concatenate(
                [
                    buf[lists_ref[t, 2 * p + i] * parts + j]
                    for i in range(2)
                    for j in range(parts)
                ],
                axis=0,
            )

        def tile_body(t, _):
            here = pl.ds(pl.multiple_of(t * TILE, TILE), TILE)

            def score_pair(p, top):
                s = lax.dot_general(
                    q_buf[here, :],
                    listed(k_buf, t, p),
                    (((1,), (1,)), ((), ())),
                    preferred_element_type=jnp.float32,
                )
                s = jnp.concatenate(
                    [
                        s[:, i * TILE : (i + 1) * TILE] * scale + bias_ref[t, 2 * p + i, g]
                        for i in range(2)
                    ],
                    axis=1,
                )
                s_buf[p] = s
                for c in range(2 * TILE // DH):
                    top = jnp.maximum(top, s[:, c * DH : (c + 1) * DH])
                return top

            top = lax.fori_loop(0, pairs, score_pair, jnp.full((TILE, DH), -3e38, jnp.float32))
            top = jnp.broadcast_to(jnp.max(top, axis=1, keepdims=True), (TILE, DH))
            acc[...] = jnp.zeros((TILE, 2 * DH), jnp.float32)

            def mix_pair(p, top):
                wide = jnp.concatenate([top] * (2 * TILE // DH), axis=1)
                weights = jnp.exp2(s_buf[p] - wide).astype(jnp.bfloat16)
                value = jnp.concatenate([listed(v_buf, t, p), ones], axis=1)
                acc[...] += jnp.dot(weights, value, preferred_element_type=jnp.float32)
                return top

            lax.fori_loop(0, pairs, mix_pair, top)
            o_buf[here, :] = (acc[:, :DH] / acc[:, DH:]).astype(jnp.bfloat16)
            return 0

        lax.fori_loop(0, frame // TILE, tile_body, 0)

    for g in range(groups):
        if g + 1 < groups:
            relay(g + 1)
        if g + 2 < groups:
            start_halo(g + 2, range(1))
        for which in range(3):
            local(which, g).wait()
        for d in range(1, n):
            across(2, g, d).wait_recv()
        for way, present in ((0, has_down), (1, has_up)):
            @pl.when(present)
            def _():
                for d in range(n):
                    for which in range(2):
                        halo(which, g, d, way).wait_recv()
        compute(g)
        for d in range(1, n):
            give(g, d).start()
        keep(g).start()

    for g in range(groups):
        for d in range(1, n):
            for which in range(3):
                across(which, g, d).wait_send()
            give(g, d).wait()
        keep(g).wait()
        for way, present in ((0, has_up), (1, has_down)):
            @pl.when(present)
            def _():
                for d in range(n):
                    for which in range(2):
                        halo(which, g, d, way).wait_send()


def on_device(queries, keys, values, rel_bias, tile_lists, tile_pos):
    n = lax.axis_size("ulysses")
    blk_count = lax.axis_size("blk")
    blk_rank = lax.axis_index("blk")
    rank = lax.axis_index("ulysses")
    groups = H // n
    tokens = queries.shape[0]
    frame_tokens = tokens * n
    frame_tiles = frame_tokens // TILE
    total_tiles, slots = tile_lists.shape

    my_lists = lax.dynamic_slice_in_dim(tile_lists, blk_rank * frame_tiles, frame_tiles, 0)
    valid = my_lists < total_tiles
    own = blk_rank * frame_tiles + jnp.arange(frame_tiles, dtype=jnp.int32)[:, None]
    safe = jnp.where(valid, my_lists, own)
    local = safe - (blk_rank - 1) * frame_tiles
    key_cell = tile_pos[safe]
    query_cell = lax.dynamic_slice_in_dim(tile_pos, blk_rank * frame_tiles, frame_tiles, 0)[:, None]
    offset = (safe // frame_tiles - blk_rank + 1) * 9
    offset = offset + (key_cell // GW - query_cell // GW + 1) * 3
    offset = offset + (key_cell % GW - query_cell % GW + 1)
    offset = jnp.clip(offset, 0, 26)
    table = lax.dynamic_slice_in_dim(rel_bias, rank * groups, groups, 0) * LOG2E
    bias = jnp.transpose(table[:, offset], (1, 2, 0))
    bias = jnp.where(valid[:, :, None], bias, -1e30)

    smem = pl.BlockSpec(memory_space=pltpu.SMEM)
    hbm = pl.BlockSpec(memory_space=pl.ANY)
    vmem = lambda *shape: [pltpu.VMEM((*shape, DH), jnp.bfloat16)] * groups
    unit = math.gcd(tokens, TILE)
    split = (tokens // unit, unit, queries.shape[1])
    dma = pltpu.SemaphoreType.DMA
    return pl.pallas_call(
        functools.partial(attention_kernel, n, blk_count, groups, tokens, slots),
        out_shape=jax.ShapeDtypeStruct(queries.shape, jnp.bfloat16),
        in_specs=[smem, smem, hbm, hbm, hbm],
        out_specs=hbm,
        scratch_shapes=[
            *vmem(3 * frame_tokens // unit, unit),
            *vmem(3 * frame_tokens // unit, unit),
            *vmem(frame_tokens),
            *vmem(frame_tokens),
            pltpu.VMEM((slots // 2, TILE, 2 * TILE), jnp.float32),
            pltpu.VMEM((TILE, 2 * DH), jnp.float32),
            dma((3, groups)),
            dma((3, groups, n)),
            dma((3, groups, n)),
            dma((2, 2, groups, n)),
            dma((2, 2, groups, n)),
            dma((groups, n)),
            dma((groups, n)),
        ],
        compiler_params=pltpu.CompilerParams(
            collective_id=0, has_side_effects=True, vmem_limit_bytes=56 * 1024 * 1024
        ),
        name="attend",
    )(local, bias, queries, keys.reshape(split), values.reshape(split))


def solution(mesh):
    return jax.shard_map(
        on_device,
        mesh=mesh,
        in_specs=(
            P(("dp", "blk", "ulysses"), None),
            P(("dp", "blk", "ulysses"), None),
            P(("dp", "blk", "ulysses"), None),
            P(),
            P(),
            P(),
        ),
        out_specs=P(("dp", "blk", "ulysses"), None),
        check_vma=False,
    )
```

time: 780 us -> 170 us (0.22)
  waiting for transfers between devices: 173 us -> 0 us
  matrix products: 162 us -> 0 us
  Pallas kernels: 0 us -> 159 us
  loops' own time: 155 us -> 0 us
  local copies, waits for them, and re-layouts: 146 us -> 7.09 us
  other arithmetic: 69.4 us -> 2.21 us
  blocking collectives: 36.1 us -> 0 us
  starting transfers between devices: 22.9 us -> 0 us
  between operations: 10.5 us -> 0.03 us
    dot_general x64 -> x0, matrix products: 162 us -> none  [the longest x32 87.1 us: attend(): jnp.einsum('ihd,jhd->hij', q_tiles[tile_slot], key_block, preferred_eleme...]
    pallas_call x0 -> x1, Pallas kernels: none -> 159 us  [on_device(): pl.pallas_call(functools.partial(attention_kernel, n, blk_count, groups,...]
    another operation x1 -> x0, loops' own time: 155 us -> none  [on_device(): final_state = lax.fori_loop(0, live_slots, by_slot, initial)]
    ppermute x2 -> x0, waiting for transfers between devices: 86.5 us -> none  [the longest x1 82.7 us: with_halo(): lax.ppermute(tail, axis, [(i, (i + 1) % count) for i in range(ends)])]
    all_to_all x3 -> x0, waiting for transfers between devices: 86.2 us -> none  [the longest x1 32.4 us: on_device(): lax.all_to_all(values, 'ulysses', split_axis=1, concat_axis=0, tiled=True)]
    while x258 -> x0, local copies, waits for them, and re-layouts: 53.3 us -> none  [the longest x2 27.1 us: on_device(): final_state = lax.fori_loop(0, live_slots, by_slot, initial)]
    slice x16 -> x0, local copies, waits for them, and re-layouts: 44.9 us -> none  [the longest x8 40.1 us: fetch(): block[1].reshape(TILE, heads_dev, DH)]
    reduce_sum x33 -> x0, other arithmetic: 42.8 us -> none  [the longest x32 42.7 us: attend(): new_total = old_total * rescale + jnp.sum(weights, axis=2)]
  transfers between devices with their start and end apart: 5 -> 0, of which waited for: 5 -> 0; matrix products, arithmetic and copies ran while one was open for 2% -> 0% of each run, Pallas kernels for 0% -> 0%
where the time goes in v1:
time: 170 us; the launch traced here: 168 us
  Pallas kernels  159 us (94%)
  local copies, waits for them, and re-layouts  7.09 us (4%)
  other arithmetic  2.21 us (1%)
    pallas_call x1, Pallas kernels, on_device(): pl.pallas_call(functools.partial(attention_kernel, n, blk_count, groups,...  159 us
    unnamed x5, local copies, waits for them, and re-layouts  4.15 us

profile of v1, /device:TPU:8, one launch (start us, length us, event | category | flops | bytes accessed | tf_op | source)
XLA Modules:
  0.0 168.2 jit_solution(10988181882534778147)
XLA Ops:
  0.0 0.0 copy-start
  0.0 0.7 and_select_fusion.1
  0.8 0.8 constant_dynamic-slice_fusion.1
  1.5 0.1 copy.11
  1.6 0.1 add_select_fusion.2
  1.7 0.1 reshape.42
  1.8 1.4 gather_fusion
  3.1 0.1 reshape.41
  3.2 0.7 compare_select_fusion
  3.9 0.1 reshape.50
  4.0 0.0 copy-done
  4.0 0.1 copy.12
  4.1 0.6 gather_fusion.1
  4.7 0.7 bitcast_select_fusion.refs_1_
  5.4 158.9 %attend.1 = bf16[768,2048]{1,0:T(8,128)(2,1)} custom-call(s32[4,8]{1,0:T(4,128)} %get-tuple-element.8.refs_0_, f32[4,8,8]{2,1,0:T(8,128)} %bitcast_select_fusion.refs_1_, bf16[768,2048]{1,0:T(8,128)(2,1)} %refs_2_.1, bf16[2,384,2048]{2,1,0:T(8,128)(2,1)} %bitcast.4, bf16[2,384,2048]{2,1,0:T(8,128)(2,1)} %bitcast.5), custom_call_target="tpu_custom_call" | custom-call | tf_op jit(solution)/shard_map/attend/pallas_call | solution.py:265
  164.2 4.0 %copy.14 = bf16[768,2048]{1,0:T(8,128)(2,1)} copy(bf16[768,2048]{1,0:T(8,128)(2,1)} %attend.1) | data formatting | bytes 6291456
  (6 shorter events, 0.0 us)
Async XLA Ops:
  0.0 4.0 %copy-start = (f32[16,27]{1,0:T(8,128)S(1)}, f32[16,27]{1,0:T(8,128)}, u32[]{:S(2)}) copy-start(f32[16,27]{1,0:T(8,128)} %param.9) | copy-start | bytes 5188
